TPU v7x, 256 devices: a whole 4x4x8 slice. The times are simulated.
256 devices in a mesh: mem: 32 (over y, z_lo, core), tile: 8 (over x, z_hi).
Axes of the slice: x: 4, y: 4, z: 8 (z_hi: 2, z_lo: 4; z = z_hi * 4 + z_lo), core: 2. Of those that a mesh axis runs over, the one named last changes fastest.
Arguments:
- weights: float32 [32, 8, 128, 512], P('mem', None, 'tile'), may hold values from -3 to 3
- perturb: bfloat16 [32, 8, 128, 512], P('mem', None, 'tile'), may hold values from -6 to 6
- coef_lon: float32 [8, 128, 512], P(None, 'tile'), may hold values from 0.01 to 0.09
- coef_lat: float32 [8, 128, 512], P(None, 'tile'), may hold values from 0.2 to 0.4
- obs_value: float32 [16384, 128], P(('mem', 'tile')), may hold values from -6 to 6
- obs_weight: float32 [16384, 128], P(('mem', 'tile')), may hold values from 0.25 to 4
- obs_segment: int32 [16384], P(('mem', 'tile')), may hold values from 0 to 511
- obs_kind: int32 [16384], P(('mem', 'tile')), may hold values from 0 to 3
- obs_target: int32 [16384, 1], P(('mem', 'tile')), may hold values from 0 to 7; in each aligned block of 64 rows (0 to 63, 64 to 127, ...) at most 16 rows name the same one
- obs_count: int32 [256], P(('mem', 'tile')), may hold values from 1 to 64, 8192 in all
- operators: float32 [4, 128, 128], replicated, may hold values from -0.5 to 0.5
Outputs:
- increment: float32 [8, 128, 512], P(None, 'tile')
- gradient: float32 [32, 8, 128, 512], P('mem', None, 'tile')
Inputs may be any that keep to these rules, and one draw needn't show every extreme that they name: `obs_target`: in the 64 rows of one owner no tile is named by more than 16 rows. The first obs_count slots of an owner hold observations, the others are empty and ignored.
All inputs are finite; a program needn't handle non-finite values. No bound on the sum of `obs_count` on one device may be relied on, other than what follows from the above.
Results may differ from a plain program's by a relative error of at most 0.0003.
Values sent between devices are 32-bit elements; how exact they have to be, the bound alone decides.
A program may use at most 64 MiB of HBM per device.

v0:
```python
import math
import jax
import jax.numpy as jnp
from jax import lax
from jax.sharding import PartitionSpec as P

SEG = 128
SWEEPS = 16


def extended_2(shard, sides, width):
    for axis, dim in sides:
        peers, length = (lax.axis_size(axis), shard.shape[dim])
        up = [(i, (i + 1) % peers) for i in range(peers - 1)]
        down = [(j, i) for i, j in up]
        last = lax.slice_in_dim(shard, length - width, length, axis=dim)
        first = lax.slice_in_dim(shard, 0, width, axis=dim)
        before = lax.ppermute(last, axis, up)
        after = lax.ppermute(first, axis, down)
        shard = jnp.concatenate([before, shard, after], axis=dim)
    return shard


def advance(current, padded, coef_lon, coef_lat):
    zonal_term = jnp.roll(current, 1, 2) + jnp.roll(current, -1, 2) - 2.0 * current
    across = padded[:, 2:] + padded[:, :-2] - 2.0 * current
    return current + coef_lon * zonal_term + coef_lat * across


def retreat(current, padded_lat, coef_lon, coef_lat):
    flux_lon = coef_lon * current
    retain = 1.0 - 2.0 * coef_lon - 2.0 * coef_lat
    return (
        retain * current
        + jnp.roll(flux_lon, 1, 2)
        + jnp.roll(flux_lon, -1, 2)
        + padded_lat[:, 2:]
        + padded_lat[:, :-2]
    )


def smooth_forward(current, coef_lon, coef_lat):
    for sweep_index in range(SWEEPS):
        padded = extended_2(current, (("tile", 1),), 1)
        current = advance(current, padded, coef_lon, coef_lat)
    return current


def smooth_adjoint(current, coef_lon, coef_lat):
    for sweep_index in range(SWEEPS):
        padded = extended_2(coef_lat * current, (("tile", 1),), 1)
        current = retreat(current, padded, coef_lon, coef_lat)
    return current


def observe(blocks, operators, kinds, values, precisions):
    images = jnp.einsum("bj,kij->kbi", blocks, operators, precision=lax.Precision.HIGHEST)
    choose = (kinds[None, :] == jnp.arange(operators.shape[0])[:, None]).astype(jnp.float32)[
        :, :, None
    ]
    modelled = jnp.sum(choose * images, 0)
    misfit = precisions * (modelled - values)
    return jnp.einsum(
        "kbi,kij->bj", choose * misfit[None], operators, precision=lax.Precision.HIGHEST
    )


def shards(
    weights,
    perturb,
    coef_lon,
    coef_lat,
    obs_value,
    obs_weight,
    obs_segment,
    obs_kind,
    obs_target,
    obs_count,
    operators,
):
    tiles = lax.axis_size("tile")
    scale = 1.0 / math.sqrt(lax.axis_size("mem"))
    member_weights = weights[0]
    member_perturb = perturb[0].astype(jnp.float32)
    product = member_perturb * smooth_forward(member_weights, coef_lon, coef_lat)
    summed = lax.psum(product, "mem")
    increment = summed * scale
    table = increment.reshape(-1, SEG)
    slots = obs_value.shape[0]
    capacity = 2 * slots // tiles
    live = jnp.arange(slots) < obs_count[0]
    target = obs_target[:, 0]
    onehot = (target[:, None] == jnp.arange(tiles)[None, :]).astype(jnp.int32)
    earlier = jnp.cumsum(onehot, 0) - onehot
    position = target * capacity + jnp.sum(earlier * onehot, 1)
    live_weight = obs_weight * live.astype(jnp.float32)[:, None]
    request = (
        jnp.full((tiles * capacity,), -1, jnp.int32)
        .at[position]
        .set(jnp.where(live, obs_segment, -1))
    )
    asked = lax.all_to_all(
        request.reshape(tiles, capacity), "tile", split_axis=0, concat_axis=0, tiled=True
    ).reshape(-1)
    valid = (asked >= 0).astype(jnp.float32)[:, None]
    index = jnp.maximum(asked, 0)
    found = table[index] * valid
    answered = lax.all_to_all(
        found.reshape(tiles, capacity, SEG), "tile", split_axis=0, concat_axis=0, tiled=True
    ).reshape(-1, SEG)
    adjoint = observe(answered[position], operators, obs_kind, obs_value, live_weight)
    outgoing = jnp.zeros((tiles * capacity, SEG), jnp.float32).at[position].set(adjoint)
    returned = lax.all_to_all(
        outgoing.reshape(tiles, capacity, SEG), "tile", split_axis=0, concat_axis=0, tiled=True
    ).reshape(-1, SEG)
    local_table = jnp.zeros_like(table).at[index].add(returned)
    adjoint_table = lax.psum(local_table, "mem")
    adjoint_field = adjoint_table.reshape(increment.shape)
    backward = smooth_adjoint(member_perturb * adjoint_field, coef_lon, coef_lat)
    member_gradient = member_weights + backward * scale
    return (increment, member_gradient[None])


def solution(mesh):
    placed = (
        P("mem", None, "tile", None),
        P("mem", None, "tile", None),
        P(None, "tile", None),
        P(None, "tile", None),
        P(("mem", "tile"), None),
        P(("mem", "tile"), None),
        P(("mem", "tile")),
        P(("mem", "tile")),
        P(("mem", "tile"), None),
        P(("mem", "tile")),
        P(),
    )
    return jax.shard_map(
        shards,
        mesh=mesh,
        in_specs=placed,
        out_specs=(P(None, "tile", None), P("mem", None, "tile", None)),
        check_vma=False,
    )
```

profile of v0, /device:TPU:6, one launch (start us, length us, event | category | flops | bytes accessed | tf_op | source)
XLA Modules:
  0.0 1062.2 jit_solution(6415799808595329105)
XLA Ops:
  12.3 11.4 %all-to-all-start = ((s32[8,1,16]{2,1,0:T(1,128)}), s32[8,1,16]{2,1,0:T(1,128)S(1)}, u32[]{:S(2)}, u32[]{:S(2)}) async-start(s32[8,1,16]{2,1,0:T(1,128)} %bitcast.7), calls=%async_computation | async-start | bytes 8192 | tf_op jit(solution)/shard_map/all_to_all | solution.py:102
  119.2 7.8 collective-permute-start.13
  132.0 7.8 collective-permute-start.15
  144.9 7.8 collective-permute-start.17
  170.6 7.8 collective-permute-start.21
  183.3 7.8 collective-permute-start.23
  196.1 7.8 collective-permute-start.25
  208.9 7.8 collective-permute-start.27
  221.6 7.8 collective-permute-start.29
  234.4 8.0 collective-permute-start.31
  246.0 278.6 %all-reduce.3.cloned.1.call-done = f32[8,16,512]{2,1,0:T(8,128)} async-done(((f32[8,16,512]{2,1,0:T(8,128)}), f32[8,16,512]{2,1,0:T(8,128)}) %all-reduce.3.cloned.1.call-update) | async-done | bytes 262160 | tf_op jit(solution)/shard_map/psum | solution.py:86
  527.6 9.8 all-to-all-start.1
  537.4 8.3 all-to-all-done.1
  548.2 12.6 %all_to_all.19 = f32[8,16,128]{2,1,0:T(8,128)S(1)} all-to-all(f32[8,16,128]{2,1,0:T(8,128)S(1)} %bitcast.56), channel_id=1, replica_groups=mesh['mem'=32,'tile'=8] {'tile'}, dimensions={0} | all-to-all | bytes 131072 | tf_op jit(solution)/shard_map/all_to_all | solution.py:113
  563.0 271.7 %all-reduce.5.cloned.1.call-done = f32[8,16,512]{2,1,0:T(8,128)} async-done(((f32[8,16,512]{2,1,0:T(8,128)}), f32[8,16,512]{2,1,0:T(8,128)}) %all-reduce.5.cloned.1.call-update) | async-done | bytes 262160 | tf_op jit(solution)/shard_map/psum | solution.py:117
  845.8 8.3 collective-permute-done.33
  856.3 8.0 collective-permute-start.35
  886.7 7.8 collective-permute-start.39
  942.4 7.8 collective-permute-start.47
  968.0 7.8 collective-permute-start.51
  980.7 7.8 collective-permute-start.53
  1006.0 7.8 collective-permute-start.57
  1018.7 7.8 collective-permute-start.59
  1031.3 7.8 collective-permute-start.61
  (304 shorter events, 311.9 us)
Async XLA Ops:
  12.3 23.8 %all-to-all-start = ((s32[8,1,16]{2,1,0:T(1,128)}), s32[8,1,16]{2,1,0:T(1,128)S(1)}, u32[]{:S(2)}, u32[]{:S(2)}) async-start(s32[8,1,16]{2,1,0:T(1,128)} %bitcast.7), calls=%async_computation | async-start | bytes 8192 | tf_op jit(solution)/shard_map/all_to_all | solution.py:102
  23.7 500.8 %all-reduce.3.cloned.1.call-start = ((), (), s32[]{:S(2)}) async-start(), calls=%async_computation.3 | async-start | bytes 524288 | tf_op jit(solution)/shard_map/psum | solution.py:86
  24.7 11.5 %collective-permute-start = (f32[8,1,512]{2,1,0:T(1,128)S(1)}, f32[8,1,512]{2,1,0:T(1,128)S(1)}, u32[]{:S(2)}, u32[]{:S(2)}) collective-permute-start(f32[8,1,512]{2,1,0:T(1,128)S(1)} %get-tuple-element.225), channel_id=1, source_target_pairs={{1,0},{2,1},{3,2},{4,3},{5,4},{6,5},{7,6},{9,8},{10,9},{11,10},{12... | collective-permute-start | bytes 49160 | tf_op jit(solution)/shard_map/ppermute | solution.py:19
  32.3 10.4 collective-permute-start.1
  45.4 10.5 collective-permute-start.3
  62.9 10.4 collective-permute-start.5
  76.0 10.4 collective-permute-start.7
  93.4 10.4 collective-permute-start.9
  106.5 10.4 collective-permute-start.11
  119.2 10.4 collective-permute-start.13
  132.0 10.6 collective-permute-start.15
  157.8 10.4 collective-permute-start.19
  170.6 10.4 collective-permute-start.21
  183.3 10.4 collective-permute-start.23
  234.4 10.6 collective-permute-start.31
  527.6 18.1 %all-to-all-start.1 = ((f32[8,16,128]{2,1,0:T(8,128)}), f32[8,16,128]{2,1,0:T(8,128)S(1)}, u32[]{:S(2)}, u32[]{:S(2)}) async-start(f32[8,16,128]{2,1,0:T(8,128)} %broadcast_multiply_fusion.1), calls=%async_computation.1 | async-start | bytes 131072 | tf_op jit(solution)/shard_map/all_to_all | solution.py:108
  537.4 297.4 %all-reduce.5.cloned.1.call-start = ((), (), s32[]{:S(2)}) async-start(), calls=%async_computation.4 | async-start | bytes 524288 | tf_op jit(solution)/shard_map/psum | solution.py:117
  843.6 10.5 collective-permute-start.33
  856.3 10.5 collective-permute-start.35
  874.1 10.4 collective-permute-start.37
  955.3 10.4 collective-permute-start.49
  968.0 10.4 collective-permute-start.51
  1006.0 10.4 collective-permute-start.57
  1018.7 10.4 collective-permute-start.59
  (54 other events, 1047.4 us)
Sparse Core Ops, SparseCore 0:
  246.1 278.4 all-reduce.2
  563.1 271.5 all-reduce.4
where the time goes:
time: 1070 us; the launch traced here: 1060 us
  waiting for transfers between devices  668 us (62%)
  starting transfers between devices  333 us (31%)
  between operations  16.2 us (2%)
  other arithmetic  16.1 us (2%)
  local copies, waits for them, and re-layouts  15.4 us (1%)
  blocking collectives  12.6 us (1%)
    psum x1, waiting for transfers between devices, shards(): summed = lax.psum(product, 'mem')  279 us
    psum x1, waiting for transfers between devices, shards(): adjoint_table = lax.psum(local_table, 'mem')  272 us
    ppermute x32, starting transfers between devices, extended_2(): before = lax.ppermute(last, axis, up)  219 us
    ppermute x32, waiting for transfers between devices, extended_2(): before = lax.ppermute(last, axis, up)  109 us
    ppermute x32, starting transfers between devices, extended_2(): after = lax.ppermute(first, axis, down)  93.7 us
  transfers between devices with their start and end apart: 68, of which 35 were waited for; matrix products, arithmetic and copies ran while one was open for 1% of the time, Pallas kernels for 0%

commit v1 on v0

--- a/solution.py
+++ b/solution.py
@@ -114,7 +114,7 @@
         outgoing.reshape(tiles, capacity, SEG), "tile", split_axis=0, concat_axis=0, tiled=True
     ).reshape(-1, SEG)
     local_table = jnp.zeros_like(table).at[index].add(returned)
-    adjoint_table = lax.psum(local_table, "mem")
+    adjoint_table = jnp.sum(lax.all_gather(local_table, "mem"), axis=0)
     adjoint_field = adjoint_table.reshape(increment.shape)
     backward = smooth_adjoint(member_perturb * adjoint_field, coef_lon, coef_lat)
     member_gradient = member_weights + backward * scale

time: 1070 us -> 861 us (0.80)
  waiting for transfers between devices: 668 us -> 458 us
    psum x1 -> x0, waiting for transfers between devices: 272 us -> none  [shards(): adjoint_table = lax.psum(local_table, 'mem')]
    all_gather x0 -> x1, waiting for transfers between devices: none -> 62.9 us  [shards(): adjoint_table = jnp.sum(lax.all_gather(local_table, 'mem'), axis=0)]
where the time goes in v1:
time: 861 us; the launch traced here: 858 us
  waiting for transfers between devices  458 us (53%)
  starting transfers between devices  333 us (39%)
  other arithmetic  23.5 us (3%)
  between operations  16.2 us (2%)
  local copies, waits for them, and re-layouts  14.3 us (2%)
  blocking collectives  12.7 us (1%)
    psum x1, waiting for transfers between devices, shards(): summed = lax.psum(product, 'mem')  279 us
    ppermute x32, starting transfers between devices, extended_2(): before = lax.ppermute(last, axis, up)  218 us
    ppermute x32, waiting for transfers between devices, extended_2(): before = lax.ppermute(last, axis, up)  108 us
    ppermute x32, starting transfers between devices, extended_2(): after = lax.ppermute(first, axis, down)  93.8 us
    all_gather x1, waiting for transfers between devices, shards(): adjoint_table = jnp.sum(lax.all_gather(local_table, 'mem'), axis=0)  62.9 us
  transfers between devices with their start and end apart: 68, of which 35 were waited for; matrix products, arithmetic and copies ran while one was open for 1% of the time, Pallas kernels for 0%

profile of v1, /device:TPU:6, one launch (start us, length us, event | category | flops | bytes accessed | tf_op | source)
XLA Modules:
  0.0 858.3 jit_solution(18401699338769374469)
XLA Ops:
  12.4 11.4 %all-to-all-start = ((s32[8,1,16]{2,1,0:T(1,128)}), s32[8,1,16]{2,1,0:T(1,128)S(1)}, u32[]{:S(2)}, u32[]{:S(2)}) async-start(s32[8,1,16]{2,1,0:T(1,128)} %bitcast.7), calls=%async_computation | async-start | bytes 8192 | tf_op jit(solution)/shard_map/all_to_all | solution.py:102
  123.5 7.8 collective-permute-start.13
  136.2 7.8 collective-permute-start.15
  149.2 7.8 collective-permute-start.17
  174.8 7.8 collective-permute-start.21
  187.6 7.8 collective-permute-start.23
  200.3 7.8 collective-permute-start.25
  213.1 7.8 collective-permute-start.27
  225.9 7.8 collective-permute-start.29
  238.6 7.8 collective-permute-start.31
  250.1 278.5 %all-reduce.2.cloned.1.call-done = f32[8,16,512]{2,1,0:T(8,128)} async-done(((f32[8,16,512]{2,1,0:T(8,128)}), f32[8,16,512]{2,1,0:T(8,128)}) %all-reduce.2.cloned.1.call-update) | async-done | bytes 262160 | tf_op jit(solution)/shard_map/psum | solution.py:86
  531.0 9.8 %all-to-all-start.1 = ((f32[8,16,128]{2,1,0:T(8,128)}), f32[8,16,128]{2,1,0:T(8,128)S(1)}, u32[]{:S(2)}, u32[]{:S(2)}) async-start(f32[8,16,128]{2,1,0:T(8,128)} %broadcast_multiply_fusion.1), calls=%async_computation.1 | async-start | bytes 131072 | tf_op jit(solution)/shard_map/all_to_all | solution.py:108
  540.8 8.2 all-to-all-done.1
  551.1 12.7 %all_to_all.19 = f32[8,16,128]{2,1,0:T(8,128)S(1)} all-to-all(f32[8,16,128]{2,1,0:T(8,128)S(1)} %bitcast.58), channel_id=1, replica_groups=mesh['mem'=32,'tile'=8] {'tile'}, dimensions={0} | all-to-all | bytes 131072 | tf_op jit(solution)/shard_map/all_to_all | solution.py:113
  565.8 62.9 %all-gather.3.cloned.1.call-done = f32[16384,128]{1,0:T(8,128)} async-done(((f32[512,128]{1,0:T(8,128)}), f32[16384,128]{1,0:T(8,128)}) %all-gather.3.cloned.1.call-update) | async-done | bytes 8388624 | tf_op jit(solution)/shard_map/all_gather | solution.py:117
  726.0 7.8 collective-permute-start.45
  738.6 7.8 collective-permute-start.47
  751.4 7.8 collective-permute-start.49
  764.1 7.8 collective-permute-start.51
  776.8 7.8 collective-permute-start.53
  789.5 7.8 collective-permute-start.55
  802.1 7.8 collective-permute-start.57
  827.5 7.8 collective-permute-start.61
  840.2 7.8 collective-permute-start.63
  (301 shorter events, 317.9 us)
Async XLA Ops:
  12.4 25.0 %all-to-all-start = ((s32[8,1,16]{2,1,0:T(1,128)}), s32[8,1,16]{2,1,0:T(1,128)S(1)}, u32[]{:S(2)}, u32[]{:S(2)}) async-start(s32[8,1,16]{2,1,0:T(1,128)} %bitcast.7), calls=%async_computation | async-start | bytes 8192 | tf_op jit(solution)/shard_map/all_to_all | solution.py:102
  23.8 504.8 %all-reduce.2.cloned.1.call-start = ((), (), s32[]{:S(2)}) async-start(), calls=%async_computation.3 | async-start | bytes 524288 | tf_op jit(solution)/shard_map/psum | solution.py:86
  24.8 12.6 %collective-permute-start = (f32[8,1,512]{2,1,0:T(1,128)S(1)}, f32[8,1,512]{2,1,0:T(1,128)S(1)}, u32[]{:S(2)}, u32[]{:S(2)}) collective-permute-start(f32[8,1,512]{2,1,0:T(1,128)S(1)} %get-tuple-element.225), channel_id=1, source_target_pairs={{1,0},{2,1},{3,2},{4,3},{5,4},{6,5},{7,6},{9,8},{10,9},{11,10},{12... | collective-permute-start | bytes 49160 | tf_op jit(solution)/shard_map/ppermute | solution.py:19
  32.3 10.4 %collective-permute-start.1 = (f32[8,1,512]{2,1,0:T(1,128)S(1)}, f32[8,1,512]{2,1,0:T(1,128)S(1)}, u32[]{:S(2)}, u32[]{:S(2)}) collective-permute-start(f32[8,1,512]{2,1,0:T(1,128)S(1)} %get-tuple-element.226), channel_id=1, source_target_pairs={{0,1},{1,2},{2,3},{3,4},{4,5},{5,6},{6,7},{8,9},{9,10},{10,11},{11... | collective-permute-start | bytes 49160 | tf_op jit(solution)/shard_map/ppermute | solution.py:18
  47.6 10.4 %collective-permute-start.3 = (f32[8,1,512]{2,1,0:T(1,128)S(1)}, f32[8,1,512]{2,1,0:T(1,128)S(1)}, u32[]{:S(2)}, u32[]{:S(2)}) collective-permute-start(f32[8,1,512]{2,1,0:T(1,128)S(1)} %get-tuple-element.220), channel_id=1, source_target_pairs={{0,1},{1,2},{2,3},{3,4},{4,5},{5,6},{6,7},{8,9},{9,10},{10,11},{11... | collective-permute-start | bytes 49160 | tf_op jit(solution)/shard_map/ppermute | solution.py:18
  65.2 10.4 %collective-permute-start.5 = (f32[8,1,512]{2,1,0:T(1,128)S(1)}, f32[8,1,512]{2,1,0:T(1,128)S(1)}, u32[]{:S(2)}, u32[]{:S(2)}) collective-permute-start(f32[8,1,512]{2,1,0:T(1,128)S(1)} %get-tuple-element.214), channel_id=1, source_target_pairs={{0,1},{1,2},{2,3},{3,4},{4,5},{5,6},{6,7},{8,9},{9,10},{10,11},{11... | collective-permute-start | bytes 49160 | tf_op jit(solution)/shard_map/ppermute | solution.py:18
  80.2 10.4 %collective-permute-start.7 = (f32[8,1,512]{2,1,0:T(1,128)S(1)}, f32[8,1,512]{2,1,0:T(1,128)S(1)}, u32[]{:S(2)}, u32[]{:S(2)}) collective-permute-start(f32[8,1,512]{2,1,0:T(1,128)S(1)} %get-tuple-element.208), channel_id=1, source_target_pairs={{0,1},{1,2},{2,3},{3,4},{4,5},{5,6},{6,7},{8,9},{9,10},{10,11},{11... | collective-permute-start | bytes 49160 | tf_op jit(solution)/shard_map/ppermute | solution.py:18
  96.8 10.4 %collective-permute-start.9 = (f32[8,1,512]{2,1,0:T(1,128)S(1)}, f32[8,1,512]{2,1,0:T(1,128)S(1)}, u32[]{:S(2)}, u32[]{:S(2)}) collective-permute-start(f32[8,1,512]{2,1,0:T(1,128)S(1)} %get-tuple-element.202), channel_id=1, source_target_pairs={{0,1},{1,2},{2,3},{3,4},{4,5},{5,6},{6,7},{8,9},{9,10},{10,11},{11... | collective-permute-start | bytes 49160 | tf_op jit(solution)/shard_map/ppermute | solution.py:18
  110.7 10.4 %collective-permute-start.11 = (f32[8,1,512]{2,1,0:T(1,128)S(1)}, f32[8,1,512]{2,1,0:T(1,128)S(1)}, u32[]{:S(2)}, u32[]{:S(2)}) collective-permute-start(f32[8,1,512]{2,1,0:T(1,128)S(1)} %get-tuple-element.196), channel_id=1, source_target_pairs={{0,1},{1,2},{2,3},{3,4},{4,5},{5,6},{6,7},{8,9},{9,10},{10,11},{11... | collective-permute-start | bytes 49160 | tf_op jit(solution)/shard_map/ppermute | solution.py:18
  123.5 10.4 %collective-permute-start.13 = (f32[8,1,512]{2,1,0:T(1,128)S(1)}, f32[8,1,512]{2,1,0:T(1,128)S(1)}, u32[]{:S(2)}, u32[]{:S(2)}) collective-permute-start(f32[8,1,512]{2,1,0:T(1,128)S(1)} %get-tuple-element.190), channel_id=1, source_target_pairs={{0,1},{1,2},{2,3},{3,4},{4,5},{5,6},{6,7},{8,9},{9,10},{10,11},{11... | collective-permute-start | bytes 49160 | tf_op jit(solution)/shard_map/ppermute | solution.py:18
  136.2 10.6 %collective-permute-start.15 = (f32[8,1,512]{2,1,0:T(1,128)S(1)}, f32[8,1,512]{2,1,0:T(1,128)S(1)}, u32[]{:S(2)}, u32[]{:S(2)}) collective-permute-start(f32[8,1,512]{2,1,0:T(1,128)S(1)} %get-tuple-element.184), channel_id=1, source_target_pairs={{0,1},{1,2},{2,3},{3,4},{4,5},{5,6},{6,7},{8,9},{9,10},{10,11},{11... | collective-permute-start | bytes 49160 | tf_op jit(solution)/shard_map/ppermute | solution.py:18
  149.2 10.4 %collective-permute-start.17 = (f32[8,1,512]{2,1,0:T(1,128)S(1)}, f32[8,1,512]{2,1,0:T(1,128)S(1)}, u32[]{:S(2)}, u32[]{:S(2)}) collective-permute-start(f32[8,1,512]{2,1,0:T(1,128)S(1)} %get-tuple-element.178), channel_id=1, source_target_pairs={{0,1},{1,2},{2,3},{3,4},{4,5},{5,6},{6,7},{8,9},{9,10},{10,11},{11... | collective-permute-start | bytes 49160 | tf_op jit(solution)/shard_map/ppermute | solution.py:18
  162.0 10.4 %collective-permute-start.19 = (f32[8,1,512]{2,1,0:T(1,128)S(1)}, f32[8,1,512]{2,1,0:T(1,128)S(1)}, u32[]{:S(2)}, u32[]{:S(2)}) collective-permute-start(f32[8,1,512]{2,1,0:T(1,128)S(1)} %get-tuple-element.172), channel_id=1, source_target_pairs={{0,1},{1,2},{2,3},{3,4},{4,5},{5,6},{6,7},{8,9},{9,10},{10,11},{11... | collective-permute-start | bytes 49160 | tf_op jit(solution)/shard_map/ppermute | solution.py:18
  174.8 10.4 %collective-permute-start.21 = (f32[8,1,512]{2,1,0:T(1,128)S(1)}, f32[8,1,512]{2,1,0:T(1,128)S(1)}, u32[]{:S(2)}, u32[]{:S(2)}) collective-permute-start(f32[8,1,512]{2,1,0:T(1,128)S(1)} %get-tuple-element.166), channel_id=1, source_target_pairs={{0,1},{1,2},{2,3},{3,4},{4,5},{5,6},{6,7},{8,9},{9,10},{10,11},{11... | collective-permute-start | bytes 49160 | tf_op jit(solution)/shard_map/ppermute | solution.py:18
  187.6 10.4 %collective-permute-start.23 = (f32[8,1,512]{2,1,0:T(1,128)S(1)}, f32[8,1,512]{2,1,0:T(1,128)S(1)}, u32[]{:S(2)}, u32[]{:S(2)}) collective-permute-start(f32[8,1,512]{2,1,0:T(1,128)S(1)} %get-tuple-element.160), channel_id=1, source_target_pairs={{0,1},{1,2},{2,3},{3,4},{4,5},{5,6},{6,7},{8,9},{9,10},{10,11},{11... | collective-permute-start | bytes 49160 | tf_op jit(solution)/shard_map/ppermute | solution.py:18
  531.0 18.0 %all-to-all-start.1 = ((f32[8,16,128]{2,1,0:T(8,128)}), f32[8,16,128]{2,1,0:T(8,128)S(1)}, u32[]{:S(2)}, u32[]{:S(2)}) async-start(f32[8,16,128]{2,1,0:T(8,128)} %broadcast_multiply_fusion.1), calls=%async_computation.1 | async-start | bytes 131072 | tf_op jit(solution)/shard_map/all_to_all | solution.py:108
  540.8 87.9 %all-gather.3.cloned.1.call-start = ((), (), s32[]{:S(2)}) async-start(), calls=%async_computation.4 | async-start | bytes 8650752 | tf_op jit(solution)/shard_map/all_gather | solution.py:117
  638.7 10.4 %collective-permute-start.33 = (f32[8,1,512]{2,1,0:T(1,128)S(1)}, f32[8,1,512]{2,1,0:T(1,128)S(1)}, u32[]{:S(2)}, u32[]{:S(2)}) collective-permute-start(f32[8,1,512]{2,1,0:T(1,128)S(1)} %get-tuple-element.130), channel_id=1, source_target_pairs={{0,1},{1,2},{2,3},{3,4},{4,5},{5,6},{6,7},{8,9},{9,10},{10,11},{11... | collective-permute-start | bytes 49160 | tf_op jit(solution)/shard_map/ppermute | solution.py:18
  652.6 10.4 %collective-permute-start.35 = (f32[8,1,512]{2,1,0:T(1,128)S(1)}, f32[8,1,512]{2,1,0:T(1,128)S(1)}, u32[]{:S(2)}, u32[]{:S(2)}) collective-permute-start(f32[8,1,512]{2,1,0:T(1,128)S(1)} %get-tuple-element.124), channel_id=1, source_target_pairs={{0,1},{1,2},{2,3},{3,4},{4,5},{5,6},{6,7},{8,9},{9,10},{10,11},{11... | collective-permute-start | bytes 49160 | tf_op jit(solution)/shard_map/ppermute | solution.py:18
  738.6 10.5 %collective-permute-start.47 = (f32[8,1,512]{2,1,0:T(1,128)S(1)}, f32[8,1,512]{2,1,0:T(1,128)S(1)}, u32[]{:S(2)}, u32[]{:S(2)}) collective-permute-start(f32[8,1,512]{2,1,0:T(1,128)S(1)} %get-tuple-element.88), channel_id=1, source_target_pairs={{0,1},{1,2},{2,3},{3,4},{4,5},{5,6},{6,7},{8,9},{9,10},{10,11},{11... | collective-permute-start | bytes 49160 | tf_op jit(solution)/shard_map/ppermute | solution.py:18
  751.4 10.5 %collective-permute-start.49 = (f32[8,1,512]{2,1,0:T(1,128)S(1)}, f32[8,1,512]{2,1,0:T(1,128)S(1)}, u32[]{:S(2)}, u32[]{:S(2)}) collective-permute-start(f32[8,1,512]{2,1,0:T(1,128)S(1)} %get-tuple-element.82), channel_id=1, source_target_pairs={{0,1},{1,2},{2,3},{3,4},{4,5},{5,6},{6,7},{8,9},{9,10},{10,11},{11... | collective-permute-start | bytes 49160 | tf_op jit(solution)/shard_map/ppermute | solution.py:18
  764.1 10.4 %collective-permute-start.51 = (f32[8,1,512]{2,1,0:T(1,128)S(1)}, f32[8,1,512]{2,1,0:T(1,128)S(1)}, u32[]{:S(2)}, u32[]{:S(2)}) collective-permute-start(f32[8,1,512]{2,1,0:T(1,128)S(1)} %get-tuple-element.76), channel_id=1, source_target_pairs={{0,1},{1,2},{2,3},{3,4},{4,5},{5,6},{6,7},{8,9},{9,10},{10,11},{11... | collective-permute-start | bytes 49160 | tf_op jit(solution)/shard_map/ppermute | solution.py:18
  789.5 10.4 %collective-permute-start.55 = (f32[8,1,512]{2,1,0:T(1,128)S(1)}, f32[8,1,512]{2,1,0:T(1,128)S(1)}, u32[]{:S(2)}, u32[]{:S(2)}) collective-permute-start(f32[8,1,512]{2,1,0:T(1,128)S(1)} %get-tuple-element.64), channel_id=1, source_target_pairs={{0,1},{1,2},{2,3},{3,4},{4,5},{5,6},{6,7},{8,9},{9,10},{10,11},{11... | collective-permute-start | bytes 49160 | tf_op jit(solution)/shard_map/ppermute | solution.py:18
  827.5 10.4 %collective-permute-start.61 = (f32[8,1,512]{2,1,0:T(1,128)S(1)}, f32[8,1,512]{2,1,0:T(1,128)S(1)}, u32[]{:S(2)}, u32[]{:S(2)}) collective-permute-start(f32[8,1,512]{2,1,0:T(1,128)S(1)} %get-tuple-element.46), channel_id=1, source_target_pairs={{0,1},{1,2},{2,3},{3,4},{4,5},{5,6},{6,7},{8,9},{9,10},{10,11},{11... | collective-permute-start | bytes 49160 | tf_op jit(solution)/shard_map/ppermute | solution.py:18
  (52 other events, 2103.4 us)
Sparse Core Ops, SparseCore 0:
  250.2 278.3 all-reduce.1
  565.9 62.6 all-gather.2
